TPU v7x, 32 devices: a whole 2x2x4 slice. The times are simulated.
32 devices in a mesh: enc: 4 (over x, core), row: 4 (over z), col: 2 (over y).
Axes of the slice: x: 2, y: 2, z: 4, core: 2. Of those that a mesh axis runs over, the one named last changes fastest.
Arguments:
- out_grad: bfloat16 [48, 8192], P(None, ('enc', 'col')), may hold values from -6 to 6
- gate_pre: bfloat16 [48, 29568], P('enc', 'row'), may hold values from -6 to 6
- up_pre: bfloat16 [48, 29568], P('enc', 'row'), may hold values from -6 to 6
- w_gate: bfloat16 [8192, 29568], P(('enc', 'col'), 'row'), may hold values from -0.0625 to 0.0625
- w_up: bfloat16 [8192, 29568], P(('enc', 'col'), 'row'), may hold values from -0.0625 to 0.0625
- w_down: bfloat16 [29568, 8192], P('row', ('enc', 'col')), may hold values from -0.03125 to 0.03125
- w_proj: bfloat16 [12800, 8192], P(None, ('enc', 'col')), may hold values from -0.0546875 to 0.0546875
- enc_hidden: bfloat16 [192, 6400], P('row', ('enc', 'col')), may hold values from -6 to 6
- route: int32 [48], replicated, may hold values from 0 to 47, each once
- img_count: int32 [4], replicated, may hold values from 1 to 12
Outputs:
- enc_grad: bfloat16 [3200, 6400], P(None, ('enc', 'col'))
Inputs may be any that keep to these rules, and one draw needn't show every extreme that they name: route[12 * r + k] is the language row that holds slot k of row group r; every language row appears once. Slots k of row group r with k >= img_count[r] are empty.
All inputs are finite; a program needn't handle non-finite values.
Results may differ from a plain program's by a relative error of at most 0.02.
Values may be sent and summed in bfloat16 or wider, within the bound.
No kernel may reach another device: no remote copies, remote signals or barrier semaphores. Data moves between devices by JAX's collectives and lax.ppermute only.
A program may use at most 128 MiB of HBM per device.

v0:
```python
import math
import jax
import jax.numpy as jnp
from jax import lax
from jax.sharding import PartitionSpec as P

SHUF = 4
IMG = 12


def contract_last(left, right):
    return lax.dot_general(
        left, right, (((1,), (1,)), ((), ())), preferred_element_type=jnp.float32
    )


def contract_first(left, right):
    return lax.dot_general(
        left, right, (((0,), (0,)), ((), ())), preferred_element_type=jnp.float32
    )


def gate_grads(hidden_grad, gate_pre, up_pre):
    share_rows = hidden_grad.shape[0]
    offset = lax.axis_index("col") * share_rows
    gate_vals = lax.dynamic_slice_in_dim(gate_pre, offset, share_rows, 0).astype(jnp.float32)
    up_vals = lax.dynamic_slice_in_dim(up_pre, offset, share_rows, 0).astype(jnp.float32)
    squash = jax.nn.sigmoid(gate_vals)
    grad_gate = (hidden_grad * up_vals * squash * (1.0 + gate_vals * (1.0 - squash))).astype(
        jnp.bfloat16
    )
    grad_up = (hidden_grad * gate_vals * squash).astype(jnp.bfloat16)
    return (grad_gate, grad_up)


def shards(out_grad, gate_pre, up_pre, w_gate, w_up, w_down, w_proj, enc_hidden, route, img_count):
    hidden_part = contract_last(out_grad, w_down)
    enc_share = lax.psum_scatter(hidden_part, "enc", scatter_dimension=0, tiled=True)
    hidden_grad = lax.psum_scatter(enc_share, "col", scatter_dimension=0, tiled=True)
    grad_gate, grad_up = gate_grads(hidden_grad, gate_pre, up_pre)
    grad_gate, grad_up = (
        lax.all_gather(grad_gate, "col", axis=0, tiled=True),
        lax.all_gather(grad_up, "col", axis=0, tiled=True),
    )
    grad_gate, grad_up = (
        lax.all_gather(grad_gate, "enc", axis=0, tiled=True),
        lax.all_gather(grad_up, "enc", axis=0, tiled=True),
    )
    routed_gate = jnp.take(grad_gate, route, axis=0)
    routed_up = jnp.take(grad_up, route, axis=0)
    input_part = contract_last(routed_gate, w_gate) + contract_last(routed_up, w_up)
    positions = jnp.arange(route.shape[0], dtype=jnp.int32)
    alive_mask = positions % IMG < jnp.repeat(img_count, IMG)
    input_part = jnp.where(alive_mask[:, None], input_part, jnp.zeros_like(input_part))
    image_grad = lax.psum_scatter(input_part, "row", scatter_dimension=0, tiled=True).astype(
        jnp.bfloat16
    )
    shuffled_grad = lax.psum_scatter(
        contract_last(image_grad, w_proj), ("enc", "col"), scatter_dimension=1, tiled=True
    )
    feature_share = shuffled_grad.shape[1] // SHUF
    patch_grad = (
        shuffled_grad.reshape(IMG, feature_share, SHUF)
        .transpose(0, 2, 1)
        .reshape(IMG * SHUF, feature_share)
        .astype(jnp.bfloat16)
    )
    patch_total = enc_hidden.shape[0] * lax.axis_size("row")
    scale = 1.0 / math.sqrt(patch_total)
    group_term = (
        contract_first(lax.all_gather(patch_grad, ("enc", "col"), axis=1, tiled=True), enc_hidden)
        * scale
    )
    total = lax.psum(group_term.astype(jnp.bfloat16), "row")
    return total


def solution(mesh):
    placed = (
        P(None, ("enc", "col")),
        P("enc", "row"),
        P("enc", "row"),
        P(("enc", "col"), "row"),
        P(("enc", "col"), "row"),
        P("row", ("enc", "col")),
        P(None, ("enc", "col")),
        P("row", ("enc", "col")),
        P(),
        P(),
    )
    return jax.shard_map(
        shards, mesh=mesh, in_specs=placed, out_specs=P(None, ("enc", "col")), check_vma=False
    )
```

profile of v0, /device:TPU:0, one launch (start us, length us, event | category | flops | bytes accessed | tf_op | source)
XLA Modules:
  0.0 432.5 jit_solution(12022463329798389478)
XLA Ops:
  6.6 0.8 copy-done
  7.4 9.9 %fusion.25 = f32[48,7392]{1,0:T(8,128)S(1)} fusion(bf16[48,1024]{1,0:T(8,128)(2,1)S(1)} %copy-done, bf16[7392,1024]{1,0:T(8,128)(2,1)} %param.17), kind=kOutput, calls=%fused_computation.36 | convolution fusion | flops 726663168 | bytes 16656384 | tf_op jit(solution)/shard_map/dot_general | solution.py:12
  17.3 22.6 %fusion = f32[16,7392]{1,0:T(8,128)S(1)} fusion(f32[48,7392]{1,0:T(8,128)S(1)} %fusion.25), kind=kCustom, calls=%all-reduce-scatter | all-reduce-scatter fusion | flops 473089 | bytes 1892864
  40.0 1.3 collective-permute-start
  44.8 9.3 %fusion.1 = f32[8,7392]{1,0:T(8,128)S(1)} fusion(f32[12,7392]{1,0:T(8,128)S(1)} %constant_dynamic-slice_fusion), kind=kCustom, calls=%all-reduce-scatter.1 | all-reduce-scatter fusion | flops 118273 | bytes 591872
  54.1 2.4 collective-permute-start.1
  56.5 1.8 collective-permute-done.1
  58.9 6.2 %all-gather.2 = bf16[2,6,7392]{2,1,0:T(8,128)(2,1)S(1)} all-gather(bf16[1,6,7392]{2,1,0:T(8,128)(2,1)S(1)} %get-tuple-element.6), channel_id=1, replica_groups=mesh['enc'=4,'row'=4,'col'=2] {'col'}, dimensions={0}, use_global_device_ids=true | all-gather | bytes 266112 | tf_op jit(solution)/shard_map/all_gather | solution.py:43
  65.2 6.8 %all-gather = bf16[2,6,7392]{2,1,0:T(8,128)(2,1)S(1)} all-gather(bf16[1,6,7392]{2,1,0:T(8,128)(2,1)S(1)} %get-tuple-element.7), channel_id=1, replica_groups=mesh['enc'=4,'row'=4,'col'=2] {'col'}, dimensions={0}, use_global_device_ids=true | all-gather | bytes 266112 | tf_op jit(solution)/shard_map/all_gather | solution.py:42
  72.2 13.2 %all-gather.1 = bf16[4,12,7392]{2,1,0:T(8,128)(2,1)S(1)} all-gather(bf16[1,12,7392]{2,1,0:T(8,128)(2,1)S(1)} %reshape.47), channel_id=1, replica_groups=mesh['enc'=4,'row'=4,'col'=2] {'enc'}, dimensions={0}, use_global_device_ids=true | all-gather | bytes 887040 | tf_op jit(solution)/shard_map/all_gather | solution.py:46
  85.7 9.6 %all-gather.3 = bf16[4,12,7392]{2,1,0:T(8,128)(2,1)S(1)} all-gather(bf16[1,12,7392]{2,1,0:T(8,128)(2,1)S(1)} %reshape.51), channel_id=1, replica_groups=mesh['enc'=4,'row'=4,'col'=2] {'enc'}, dimensions={0}, use_global_device_ids=true | all-gather | bytes 887040 | tf_op jit(solution)/shard_map/all_gather | solution.py:47
  95.7 1.0 gather_fusion
  96.7 1.0 gather_fusion.1
  97.7 8.1 %fusion.5 = f32[48,1024]{1,0:T(8,128)S(1)} fusion(bf16[1024,7392]{0,1:T(8,128)(2,1)} %param.15, bf16[48,7392]{1,0:T(8,128)(2,1)S(1)} %gather_fusion, pred[48]{0:T(512)(128)(4,1)S(1)} %compare_and_fusion), kind=kOutput, calls=%fused_computation.7 | convolution fusion | flops 727017984 | bytes 16045104 | tf_op jit(solution)/shard_map/dot_general | solution.py:12
  105.8 8.1 %fusion.3 = f32[48,1024]{1,0:T(8,128)S(1)} fusion(f32[48,1024]{1,0:T(8,128)S(1)} %fusion.5, bf16[1024,7392]{0,1:T(8,128)(2,1)} %param.16, bf16[48,7392]{1,0:T(8,128)(2,1)S(1)} %gather_fusion.1, pred[48]{0:T(512)(128)(4,1)S(1)} %compare_and_fusion, pred[48]{0:T(512)(128)(4,1)S(1)} %fusion.22), kind=kOutput, calls=%fused_computation.5 | convolution fusion | flops 727116288 | bytes 16241760 | tf_op jit(solution)/shard_map/dot_general | solution.py:12
  114.0 15.4 %fusion.2 = f32[16,1024]{1,0:T(8,128)S(1)} fusion(f32[48,1024]{1,0:T(8,128)S(1)} %fusion.3), kind=kCustom, calls=%all-reduce-scatter.2 | all-reduce-scatter fusion | flops 65537 | bytes 262656
  129.4 2.0 collective-permute-start.2
  133.2 14.8 %convolution_bitcast_fusion = f32[12800,12]{1,0:T(8,128)} fusion(bf16[12800,1024]{1,0:T(8,128)(2,1)} %param.18, bf16[28,1024]{1,0:T(8,128)(2,1)S(1)} %concatenate.2, u32[]{:S(6)} %subtract.2), kind=kOutput, calls=%fused_computation.2 | convolution fusion | flops 314572800 | bytes 26861572
  148.1 63.3 %reduce-scatter.10.cloned.1.call-done = f32[1600,12]{1,0:T(8,128)} async-done(((f32[12800,12]{1,0:T(8,128)}), f32[1600,12]{1,0:T(8,128)}) %reduce-scatter.10.cloned.1.call-update) | async-done | bytes 76816
  211.4 1.4 copy.18
  213.5 17.0 %all-gather.4 = bf16[8,400,48]{1,2,0:T(8,128)(2,1)S(1)} all-gather(bf16[1,400,48]{1,2,0:T(8,128)(2,1)S(1)} %bitcast.33), channel_id=1, replica_groups=mesh['enc'=4,'row'=4,'col'=2] {'enc','col'}, dimensions={0}, use_global_device_ids=true | all-gather | bytes 345600 | tf_op jit(solution)/shard_map/all_gather | solution.py:71
  231.3 3.9 multiply_convert_fusion
  235.2 185.4 %all-reduce.8.cloned.1.call-done = bf16[3200,800]{0,1:T(8,128)(2,1)} async-done(((bf16[3200,800]{0,1:T(8,128)(2,1)}), bf16[3200,800]{0,1:T(8,128)(2,1)}) %all-reduce.8.cloned.1.call-update) | async-done | bytes 5120016 | tf_op jit(solution)/shard_map/psum | solution.py:74
  420.5 5.1 %copy.20 = bf16[3200,800]{0,1:T(8,128)(2,1)} copy(bf16[3200,800]{0,1:T(8,128)(2,1)} %all-reduce.8.cloned.1.call-done) | data formatting | bytes 10240000
  (51 shorter events, 6.2 us)
Async XLA Ops:
  6.5 0.9 copy-start
  6.5 34.8 %copy-start.8 = (u32[32]{0:T(128)S(1)}, u32[32]{0:T(128)}, u32[]{:S(2)}) copy-start(u32[32]{0:T(128)} %constant.41) | copy-start | bytes 388
  6.5 36.0 %copy-start.7 = (u32[32]{0:T(128)S(1)}, u32[32]{0:T(128)}, u32[]{:S(2)}) copy-start(u32[32]{0:T(128)} %constant.37) | copy-start | bytes 388
  6.5 36.6 %copy-start.9 = (s32[48]{0:T(128)S(1)}, s32[48]{0:T(128)}, u32[]{:S(2)}) copy-start(s32[48]{0:T(128)} %param.20) | copy-start | bytes 580
  6.5 36.6 %copy-start.5 = (s32[4]{0:T(128)S(1)}, s32[4]{0:T(128)}, u32[]{:S(2)}) copy-start(s32[4]{0:T(128)} %param.21) | copy-start | bytes 52
  6.5 52.1 %copy-start.4 = (bf16[12,7392]{1,0:T(8,128)(2,1)S(1)}, bf16[12,7392]{1,0:T(8,128)(2,1)}, u32[]{:S(2)}) copy-start(bf16[12,7392]{1,0:T(8,128)(2,1)} %param.14) | copy-start | bytes 532228
  6.6 52.1 %copy-start.3 = (bf16[12,7392]{1,0:T(8,128)(2,1)S(1)}, bf16[12,7392]{1,0:T(8,128)(2,1)}, u32[]{:S(2)}) copy-start(bf16[12,7392]{1,0:T(8,128)(2,1)} %param.13) | copy-start | bytes 532228
  6.6 204.9 %reduce-scatter.10.cloned.1.call-start = ((), (), s32[]{:S(2)}) async-start(), calls=%async_computation.2 | async-start | bytes 7372800
  40.0 4.0 collective-permute-start
  54.1 4.2 collective-permute-start.1
  105.8 25.7 %copy-start.6 = (u32[32]{0:T(128)S(1)}, u32[32]{0:T(128)}, u32[]{:S(2)}) copy-start(u32[32]{0:T(128)} %constant.45) | copy-start | bytes 388
  129.4 3.6 collective-permute-start.2
  133.2 98.1 %copy-start.2 = (bf16[48,800]{1,0:T(8,128)(2,1)S(1)}, bf16[48,800]{1,0:T(8,128)(2,1)}, u32[]{:S(2)}) copy-start(bf16[48,800]{1,0:T(8,128)(2,1)} %param.19) | copy-start | bytes 230404
  148.0 277.6 %copy-start.1 = (bf16[48,1024]{1,0:T(8,128)(2,1)S(1)}, bf16[48,1024]{1,0:T(8,128)(2,1)}, u32[]{:S(2)}) copy-start(bf16[48,1024]{1,0:T(8,128)(2,1)} %param.12) | copy-start | bytes 294916
  148.0 272.5 %all-reduce.8.cloned.1.call-start = ((), (), s32[]{:S(2)}) async-start(), calls=%async_computation.1 | async-start | bytes 10240000 | tf_op jit(solution)/shard_map/psum | solution.py:74
Sparse Core Ops, SparseCore 0:
  148.2 63.2 reduce-scatter.9
  235.3 185.2 all-reduce.7
where the time goes:
time: 433 us
  waiting for transfers between devices  251 us (58%)
  blocking collectives  100 us (23%)
  matrix products  44.8 us (10%)
  between operations  15.7 us (4%)
  local copies, waits for them, and re-layouts  15 us (3%)
  starting transfers between devices  5.85 us (1%)
    psum x1, waiting for transfers between devices, shards(): total = lax.psum(group_term.astype(jnp.bfloat16), 'row')  185 us
    unnamed x6, waiting for transfers between devices  65.5 us
    unnamed x3, blocking collectives  47.2 us
    dot_general x3, matrix products, contract_last(): lax.dot_general(left, right, (((1,), (1,)), ((), ())), preferred_element_...  26.1 us
    all_gather x1, blocking collectives, shards(): lax.all_gather(patch_grad, ('enc', 'col'), axis=1, tiled=True)  17 us
    unnamed x1, matrix products  14.8 us
    all_gather x1, blocking collectives, shards(): lax.all_gather(grad_gate, 'enc', axis=0, tiled=True)  13.2 us
    unnamed x37, local copies, waits for them, and re-layouts  11.9 us
  transfers between devices with their start and end apart: 5, of which 4 were waited for; matrix products, arithmetic and copies ran while one was open for 0% of the time, Pallas kernels for 0%

commit v1 on v0

--- a/solution.py
+++ b/solution.py
@@ -71,7 +71,7 @@
         contract_first(lax.all_gather(patch_grad, ("enc", "col"), axis=1, tiled=True), enc_hidden)
         * scale
     )
-    total = lax.psum(group_term.astype(jnp.bfloat16), "row")
+    total = jnp.sum(lax.all_gather(group_term.astype(jnp.bfloat16), "row"), axis=0)
     return total
 
 

time: 433 us -> 656 us (1.52)
  waiting for transfers between devices: 251 us -> 414 us
  other arithmetic: 0.23 us -> 30.5 us
  local copies, waits for them, and re-layouts: 15 us -> 43.7 us
    all_gather x0 -> x1, waiting for transfers between devices: none -> 349 us  [shards(): lax.all_gather(group_term.astype(jnp.bfloat16), 'row')]
    psum x1 -> x0, waiting for transfers between devices: 185 us -> none  [shards(): total = lax.psum(group_term.astype(jnp.bfloat16), 'row')]
    all_gather x0 -> x1, local copies, waits for them, and re-layouts: none -> 33.8 us  [shards(): lax.all_gather(group_term.astype(jnp.bfloat16), 'row')]
    reduce_sum x0 -> x1, other arithmetic: none -> 30.3 us  [shards(): jnp.sum(lax.all_gather(group_term.astype(jnp.bfloat16), 'row'), axis=0)]
where the time goes in v1:
time: 656 us; the launch traced here: 655 us
  waiting for transfers between devices  414 us (63%)
  blocking collectives  100 us (15%)
  matrix products  44.8 us (7%)
  local copies, waits for them, and re-layouts  43.7 us (7%)
  other arithmetic  30.5 us (5%)
  between operations  15.7 us (2%)
    all_gather x1, waiting for transfers between devices, shards(): lax.all_gather(group_term.astype(jnp.bfloat16), 'row')  349 us
    unnamed x6, waiting for transfers between devices  65.5 us
    unnamed x3, blocking collectives  47.2 us
    all_gather x1, local copies, waits for them, and re-layouts, shards(): lax.all_gather(group_term.astype(jnp.bfloat16), 'row')  33.8 us
    reduce_sum x1, other arithmetic, shards(): jnp.sum(lax.all_gather(group_term.astype(jnp.bfloat16), 'row'), axis=0)  30.3 us
    dot_general x3, matrix products, contract_last(): lax.dot_general(left, right, (((1,), (1,)), ((), ())), preferred_element_...  26.1 us
    all_gather x1, blocking collectives, shards(): lax.all_gather(patch_grad, ('enc', 'col'), axis=1, tiled=True)  17 us
    unnamed x1, matrix products  14.8 us
  transfers between devices with their start and end apart: 5, of which 4 were waited for; matrix products, arithmetic and copies ran while one was open for 0% of the time, Pallas kernels for 0%

profile of v1, /device:TPU:0, one launch (start us, length us, event | category | flops | bytes accessed | tf_op | source)
XLA Modules:
  0.0 655.0 jit_solution(10957209178124227281)
XLA Ops:
  7.4 9.9 %fusion.25 = f32[48,7392]{1,0:T(8,128)S(1)} fusion(bf16[48,1024]{1,0:T(8,128)(2,1)S(1)} %copy-done, bf16[7392,1024]{1,0:T(8,128)(2,1)} %param.17), kind=kOutput, calls=%fused_computation.36 | convolution fusion | flops 726663168 | bytes 16656384 | tf_op jit(solution)/shard_map/dot_general | solution.py:12
  17.3 22.6 %fusion = f32[16,7392]{1,0:T(8,128)S(1)} fusion(f32[48,7392]{1,0:T(8,128)S(1)} %fusion.25), kind=kCustom, calls=%all-reduce-scatter | all-reduce-scatter fusion | flops 473089 | bytes 1892864
  40.0 1.3 collective-permute-start
  44.8 9.3 %fusion.1 = f32[8,7392]{1,0:T(8,128)S(1)} fusion(f32[12,7392]{1,0:T(8,128)S(1)} %constant_dynamic-slice_fusion), kind=kCustom, calls=%all-reduce-scatter.1 | all-reduce-scatter fusion | flops 118273 | bytes 591872
  54.1 2.4 collective-permute-start.1
  56.5 1.8 collective-permute-done.1
  58.9 6.2 all-gather.3
  65.2 6.8 %all-gather.1 = bf16[2,6,7392]{2,1,0:T(8,128)(2,1)S(1)} all-gather(bf16[1,6,7392]{2,1,0:T(8,128)(2,1)S(1)} %get-tuple-element.7), channel_id=1, replica_groups=mesh['enc'=4,'row'=4,'col'=2] {'col'}, dimensions={0}, use_global_device_ids=true | all-gather | bytes 266112 | tf_op jit(solution)/shard_map/all_gather | solution.py:42
  72.2 13.2 %all-gather.2 = bf16[4,12,7392]{2,1,0:T(8,128)(2,1)S(1)} all-gather(bf16[1,12,7392]{2,1,0:T(8,128)(2,1)S(1)} %reshape.48), channel_id=1, replica_groups=mesh['enc'=4,'row'=4,'col'=2] {'enc'}, dimensions={0}, use_global_device_ids=true | all-gather | bytes 887040 | tf_op jit(solution)/shard_map/all_gather | solution.py:46
  85.7 9.6 %all-gather.4 = bf16[4,12,7392]{2,1,0:T(8,128)(2,1)S(1)} all-gather(bf16[1,12,7392]{2,1,0:T(8,128)(2,1)S(1)} %reshape.52), channel_id=1, replica_groups=mesh['enc'=4,'row'=4,'col'=2] {'enc'}, dimensions={0}, use_global_device_ids=true | all-gather | bytes 887040 | tf_op jit(solution)/shard_map/all_gather | solution.py:47
  95.7 1.0 gather_fusion
  96.7 1.0 gather_fusion.1
  97.7 8.1 %fusion.5 = f32[48,1024]{1,0:T(8,128)S(1)} fusion(bf16[1024,7392]{0,1:T(8,128)(2,1)} %param.15, bf16[48,7392]{1,0:T(8,128)(2,1)S(1)} %gather_fusion, pred[48]{0:T(512)(128)(4,1)S(1)} %compare_and_fusion), kind=kOutput, calls=%fused_computation.7 | convolution fusion | flops 727017984 | bytes 16045104 | tf_op jit(solution)/shard_map/dot_general | solution.py:12
  105.8 8.1 %fusion.3 = f32[48,1024]{1,0:T(8,128)S(1)} fusion(f32[48,1024]{1,0:T(8,128)S(1)} %fusion.5, bf16[1024,7392]{0,1:T(8,128)(2,1)} %param.16, bf16[48,7392]{1,0:T(8,128)(2,1)S(1)} %gather_fusion.1, pred[48]{0:T(512)(128)(4,1)S(1)} %compare_and_fusion, pred[48]{0:T(512)(128)(4,1)S(1)} %fusion.22), kind=kOutput, calls=%fused_computation.5 | convolution fusion | flops 727116288 | bytes 16241760 | tf_op jit(solution)/shard_map/dot_general | solution.py:12
  114.0 15.4 %fusion.2 = f32[16,1024]{1,0:T(8,128)S(1)} fusion(f32[48,1024]{1,0:T(8,128)S(1)} %fusion.3), kind=kCustom, calls=%all-reduce-scatter.2 | all-reduce-scatter fusion | flops 65537 | bytes 262656
  129.4 2.0 collective-permute-start.2
  133.2 14.8 %convolution_bitcast_fusion = f32[12800,12]{1,0:T(8,128)} fusion(bf16[12800,1024]{1,0:T(8,128)(2,1)} %param.18, bf16[28,1024]{1,0:T(8,128)(2,1)S(1)} %concatenate.2, u32[]{:S(6)} %subtract.2), kind=kOutput, calls=%fused_computation.2 | convolution fusion | flops 314572800 | bytes 26861572
  148.1 63.3 %reduce-scatter.10.cloned.1.call-done = f32[1600,12]{1,0:T(8,128)} async-done(((f32[12800,12]{1,0:T(8,128)}), f32[1600,12]{1,0:T(8,128)}) %reduce-scatter.10.cloned.1.call-update) | async-done | bytes 76816
  211.4 1.4 copy.18
  213.5 17.0 %all-gather.5 = bf16[8,400,48]{1,2,0:T(8,128)(2,1)S(1)} all-gather(bf16[1,400,48]{1,2,0:T(8,128)(2,1)S(1)} %bitcast.35), channel_id=1, replica_groups=mesh['enc'=4,'row'=4,'col'=2] {'enc','col'}, dimensions={0}, use_global_device_ids=true | all-gather | bytes 345600 | tf_op jit(solution)/shard_map/all_gather | solution.py:71
  231.3 3.9 multiply_convert_fusion
  235.2 349.0 %all-gather.8.cloned.1.call-done = bf16[12800,800]{0,1:T(8,128)(2,1)} async-done(((bf16[3200,800]{0,1:T(8,128)(2,1)}), bf16[12800,800]{0,1:T(8,128)(2,1)}) %all-gather.8.cloned.1.call-update) | async-done | bytes 20480016 | tf_op jit(solution)/shard_map/all_gather | solution.py:74
  584.1 33.8 %reshape.43 = bf16[4,3200,800]{1,0,2:T(4,128)(2,1)} reshape(bf16[12800,800]{0,1:T(8,128)(2,1)} %all-gather.8.cloned.1.call-done) | data formatting | bytes 40960000 | tf_op jit(solution)/shard_map/all_gather | solution.py:74
  617.9 30.3 %reduce_sum.12 = bf16[3200,800]{0,1:T(8,128)(2,1)} reduce(bf16[4,3200,800]{1,0,2:T(4,128)(2,1)} %reshape.43, bf16[]{:T(256)} %constant.37.clone.1), dimensions={0}, to_apply=%region_4.6 | reduce | flops 7680000 | bytes 25600002 | tf_op jit(solution)/shard_map/reduce_sum | solution.py:74
  (52 shorter events, 7.1 us)
Async XLA Ops:
  6.5 0.9 copy-start
  6.5 34.8 %copy-start.8 = (u32[32]{0:T(128)S(1)}, u32[32]{0:T(128)}, u32[]{:S(2)}) copy-start(u32[32]{0:T(128)} %constant.44) | copy-start | bytes 388
  6.5 36.0 %copy-start.7 = (u32[32]{0:T(128)S(1)}, u32[32]{0:T(128)}, u32[]{:S(2)}) copy-start(u32[32]{0:T(128)} %constant.40) | copy-start | bytes 388
  6.5 36.6 %copy-start.9 = (s32[48]{0:T(128)S(1)}, s32[48]{0:T(128)}, u32[]{:S(2)}) copy-start(s32[48]{0:T(128)} %param.20) | copy-start | bytes 580
  6.5 36.6 %copy-start.5 = (s32[4]{0:T(128)S(1)}, s32[4]{0:T(128)}, u32[]{:S(2)}) copy-start(s32[4]{0:T(128)} %param.21) | copy-start | bytes 52
  6.5 52.1 %copy-start.4 = (bf16[12,7392]{1,0:T(8,128)(2,1)S(1)}, bf16[12,7392]{1,0:T(8,128)(2,1)}, u32[]{:S(2)}) copy-start(bf16[12,7392]{1,0:T(8,128)(2,1)} %param.14) | copy-start | bytes 532228
  6.6 52.1 %copy-start.3 = (bf16[12,7392]{1,0:T(8,128)(2,1)S(1)}, bf16[12,7392]{1,0:T(8,128)(2,1)}, u32[]{:S(2)}) copy-start(bf16[12,7392]{1,0:T(8,128)(2,1)} %param.13) | copy-start | bytes 532228
  6.6 204.9 %reduce-scatter.10.cloned.1.call-start = ((), (), s32[]{:S(2)}) async-start(), calls=%async_computation.2 | async-start | bytes 7372800
  40.0 4.0 collective-permute-start
  54.1 4.2 collective-permute-start.1
  105.8 25.7 %copy-start.6 = (u32[32]{0:T(128)S(1)}, u32[32]{0:T(128)}, u32[]{:S(2)}) copy-start(u32[32]{0:T(128)} %constant.48) | copy-start | bytes 388
  129.4 3.6 collective-permute-start.2
  133.2 98.1 %copy-start.2 = (bf16[48,800]{1,0:T(8,128)(2,1)S(1)}, bf16[48,800]{1,0:T(8,128)(2,1)}, u32[]{:S(2)}) copy-start(bf16[48,800]{1,0:T(8,128)(2,1)} %param.19) | copy-start | bytes 230404
  148.0 436.1 %all-gather.8.cloned.1.call-start = ((), (), s32[]{:S(2)}) async-start(), calls=%async_computation.1 | async-start | bytes 25600000 | tf_op jit(solution)/shard_map/all_gather | solution.py:74
  584.1 64.1 %copy-start.1 = (bf16[48,1024]{1,0:T(8,128)(2,1)S(1)}, bf16[48,1024]{1,0:T(8,128)(2,1)}, u32[]{:S(2)}) copy-start(bf16[48,1024]{1,0:T(8,128)(2,1)} %param.12) | copy-start | bytes 294916
Sparse Core Ops, SparseCore 0:
  148.2 63.2 reduce-scatter.9
  235.3 348.7 all-gather.7
